TPU v7x, 512 devices: a whole 4x8x8 slice. The times are simulated.
512 devices in a mesh: contact: 8 (over x, core), body: 8 (over z), group: 8 (over y).
Axes of the slice: x: 4, y: 8, z: 8, core: 2. Of those that a mesh axis runs over, the one named last changes fastest.
Arguments:
- jacobian_a: float32 [18, 1835008], P(None, ('contact', 'body', 'group')), may hold values from -4 to 4
- jacobian_b: float32 [18, 1835008], P(None, ('contact', 'body', 'group')), may hold values from -4 to 4
- warm_start: float32 [3, 1835008], P(None, ('contact', 'body', 'group')), may hold values from -4 to 4
- free_gap: float32 [3, 1835008], P(None, ('contact', 'body', 'group')), may hold values from -25 to 25
- compliance: float32 [3, 1835008], P(None, ('contact', 'body', 'group')), may hold values from 0.05 to 2.5
- friction: float32 [1835008], P(('contact', 'body', 'group')), may hold values from 0.2 to 0.8
- cone_active: int32 [1835008], P(('contact', 'body', 'group')), may hold values 0 or 1
- body_index_a: int32 [1835008], P(('contact', 'body', 'group')), may hold values from 0 to 4095
- body_index_b: int32 [1835008], P(('contact', 'body', 'group')), may hold values from 0 to 4095
- block_owner: int32 [28672, 1], P(('contact', 'body', 'group')), may hold values from 0 to 63; in each aligned block of 56 rows (0 to 55, 56 to 111, ...) at most 2 rows name the same one
- inverse_mass: float32 [6, 262144], P(None, ('body', 'group')), may hold values from 0.3 to 3
- free_velocity: float32 [6, 262144], P(None, ('body', 'group')), may hold values from -6 to 6
Outputs:
- impulse: float32 [3, 1835008], P(None, ('contact', 'body', 'group'))
- velocity: float32 [6, 262144], P(None, ('body', 'group'))
Inputs may be any that keep to these rules, and one draw needn't show every extreme that they name: `block_owner`: in each aligned block of 56 rows (the contact blocks of one device) no shard is named more than 2 times.
All inputs are finite; a program needn't handle non-finite values. No bound on the sum of `cone_active` on one device may be relied on, other than what follows from the above.
Results may differ from a plain program's by a relative error of at most 0.0003.
Values sent between devices are 32-bit elements; how exact they have to be, the bound alone decides.
A program may use at most 64 MiB of HBM per device.

v0:
```python
import math
import jax
import jax.numpy as jnp
from jax import lax
from jax.sharding import Mesh
from jax.sharding import PartitionSpec as P

CBLK = 64
ITERS = 2
CONTACT = ("contact_0", "contact_1")
CONTACT_BODY_GROUP = ("contact_0", "contact_1", "body", "group")
EPS = 1e-06
SMOOTH = 0.1


def copy_for_each(array, axis):
    length = lax.axis_size(axis)
    return lax.all_to_all(
        jnp.broadcast_to(array[None], (length, *array.shape)), axis, 0, 0, tiled=True
    )


def of_everyone(array, axis):
    everything = copy_for_each(array, axis)
    return jnp.sum(everything, axis=0)


def by_axis(array, axes):
    for axis in axes:
        array = lax.psum(array, axis)
    return array


def momentum_table(iterations):
    theta_now = 1.0
    coefficients = []
    for rounds in range(iterations):
        following = 0.5 * (
            theta_now * math.sqrt(theta_now * theta_now + 4.0) - theta_now * theta_now
        )
        coefficients.append(theta_now * (1.0 - theta_now) / (theta_now * theta_now + following))
        theta_now = following
    return coefficients


def project_cone(values, friction, cone_active):
    normal = values[0]
    tangent = values[1:3]
    spread = jnp.sqrt(tangent[0] * tangent[0] + tangent[1] * tangent[1] + SMOOTH * SMOOTH)
    sticking = spread <= friction * normal
    separated = friction * spread <= -normal
    cone_normal = (normal + friction * spread) / (1.0 + friction * friction)
    shrink_factor = friction * cone_normal / spread
    new_normal = jnp.where(sticking, normal, jnp.where(separated, 0.0, cone_normal))
    new_tangent = jnp.where(
        sticking[None], tangent, jnp.where(separated[None], 0.0, shrink_factor[None] * tangent)
    )
    switched = cone_active == 1
    out_normal = jnp.where(switched, new_normal, jnp.maximum(normal, 0.0))
    out_tangent = jnp.where(switched[None], new_tangent, 0.0)
    return jnp.concatenate([out_normal[None], out_tangent], axis=0)


def impulse_terms(jacobian, values):
    return jnp.sum(jacobian.reshape(3, 6, -1) * values[:, None, :], axis=0)


def velocity_terms(jacobian, velocities):
    return jnp.sum(jacobian.reshape(3, 6, -1) * velocities[None, :, :], axis=1)


def slot_places(block_owner, capacity):
    target = block_owner[:, 0]
    matching = (target[:, None] == target[None, :]).astype(jnp.int32)
    ordinal = jnp.arange(target.shape[0], dtype=jnp.int32)
    earlier = (ordinal[None, :] < ordinal[:, None]).astype(jnp.int32)
    ranking = jnp.sum(matching * earlier, axis=1)
    return target * capacity + ranking


def pack_slots(values, places, shards, capacity):
    leading = values.shape[0]
    blocks = values.reshape(leading, -1, CBLK)
    buffer = jnp.zeros((leading, shards * capacity, CBLK), values.dtype)
    buffer = buffer.at[:, places, :].set(blocks)
    return buffer.reshape(leading, shards, capacity * CBLK)


def unpack_slots(buffer, places):
    leading = buffer.shape[0]
    blocks = buffer.reshape(leading, -1, CBLK)[:, places, :]
    return blocks.reshape(leading, -1)


def trade(buffer):
    return lax.all_to_all(buffer, ("body", "group"), split_axis=1, concat_axis=1, tiled=True)


def on_device(
    jacobian_a,
    jacobian_b,
    warm_start,
    free_gap,
    compliance,
    friction,
    cone_active,
    body_index_a,
    body_index_b,
    block_owner,
    inverse_mass,
    free_velocity,
):
    shards = lax.axis_size(("body", "group"))
    capacity = max(2, 2 * block_owner.shape[0] // shards)
    places = slot_places(block_owner, capacity)
    bodies = inverse_mass.shape[1]
    index_slots = pack_slots(body_index_b[None, :], places, shards, capacity)
    far_index = lax.all_to_all(
        index_slots, ("body", "group"), split_axis=1, concat_axis=1, tiled=True
    ).reshape(-1)

    def body_impulse(values):
        summed = (
            jnp.zeros((6, bodies), jnp.float32)
            .at[:, body_index_a]
            .add(impulse_terms(jacobian_a, values))
        )
        far_terms = trade(
            pack_slots(impulse_terms(jacobian_b, values), places, shards, capacity)
        ).reshape(6, -1)
        summed = summed.at[:, far_index].add(far_terms)
        return of_everyone(summed, CONTACT)

    momentum = momentum_table(ITERS)
    current = warm_start
    before = jnp.zeros_like(warm_start)
    gradient_before = free_gap
    latest = warm_start
    for rounds in range(ITERS):
        velocities = inverse_mass * body_impulse(current)
        near_part = velocity_terms(jacobian_a, velocities[:, body_index_a])
        returned = trade(velocities[:, far_index].reshape(6, shards, -1))
        gradient = (
            near_part
            + velocity_terms(jacobian_b, unpack_slots(returned, places))
            + compliance * current
            + free_gap
        )
        iterate_change = current - before
        gradient_change = gradient - gradient_before
        change_squares, gradient_squares = (
            by_axis(jnp.sum(iterate_change * iterate_change), CONTACT_BODY_GROUP),
            by_axis(jnp.sum(gradient_change * gradient_change), CONTACT_BODY_GROUP),
        )
        stride = jnp.sqrt((change_squares + EPS) / (gradient_squares + EPS))
        projected = project_cone(current - stride * gradient, friction, cone_active)
        following = projected + momentum[rounds] * (projected - latest)
        before, gradient_before, latest, current = (current, gradient, projected, following)
    velocity = free_velocity + inverse_mass * body_impulse(latest)
    return (latest, velocity)


def solution(mesh):
    torus = Mesh(
        mesh.devices.reshape(4, 2, mesh.shape["body"], mesh.shape["group"]),
        ("contact_0", "contact_1", "body", "group"),
    )
    placed = (
        P(None, CONTACT_BODY_GROUP),
        P(None, CONTACT_BODY_GROUP),
        P(None, CONTACT_BODY_GROUP),
        P(None, CONTACT_BODY_GROUP),
        P(None, CONTACT_BODY_GROUP),
        P(CONTACT_BODY_GROUP),
        P(CONTACT_BODY_GROUP),
        P(CONTACT_BODY_GROUP),
        P(CONTACT_BODY_GROUP),
        P(CONTACT_BODY_GROUP, None),
        P(None, ("body", "group")),
        P(None, ("body", "group")),
    )
    return jax.shard_map(
        on_device,
        mesh=torus,
        in_specs=placed,
        out_specs=(P(None, CONTACT_BODY_GROUP), P(None, ("body", "group"))),
        check_vma=False,
    )
```

profile of v0, /device:TPU:8, one launch (start us, length us, event | category | flops | bytes accessed | tf_op | source)
XLA Modules:
  0.0 576.4 jit_solution(6024349499058837542)
XLA Ops:
  0.6 0.9 select_reduce_fusion
  1.5 0.7 fusion.10
  2.2 0.8 reshape.201
  3.0 0.7 scatter_custom_fusion.1
  3.7 0.7 reshape.123
  4.4 16.6 %all-to-all-start = ((s32[1,64,128]{2,0,1:T(1,128)}), s32[1,64,128]{2,0,1:T(1,128)S(1)}, u32[]{:S(2)}, u32[]{:S(2)}) async-start(s32[1,64,128]{2,0,1:T(1,128)} %bitcast.4), calls=%async_computation | async-start | bytes 65536 | tf_op jit(solution)/shard_map/all_to_all | solution.py:118
  21.0 1.0 reshape.122
  22.0 1.0 reshape.125
  23.1 0.7 compare_select_fusion.1
  23.8 0.9 multiply_reduce_fusion.8
  24.9 2.5 scatter_fusion
  27.6 0.8 copy.196
  28.4 1.8 copy.192
  30.2 20.5 %scatter_custom_fusion = f32[6,4096]{0,1:T(8,128)S(1)} fusion(s32[3584]{0:T(1024)S(1)} %compare_select_fusion.1, f32[3584,6]{1,0:T(8,128)} %copy.192, f32[]{:T(128)} %constant.10.clone.1), kind=kCustom, calls=%fused_computation.20 | custom fusion | flops 21504 | bytes 98816 | tf_op jit(solution)/shard_map/scatter-add | solution.py:126
  50.7 12.7 %all-to-all-start.1 = ((f32[6,64,128]{2,0,1:T(8,128)}), f32[6,64,128]{2,0,1:T(8,128)S(1)}, u32[]{:S(2)}, u32[]{:S(2)}) async-start(f32[6,64,128]{2,0,1:T(8,128)} %copy.196), calls=%async_computation.1 | async-start | bytes 524288 | tf_op jit(solution)/shard_map/all_to_all | solution.py:96
  63.5 13.7 %all-to-all-done.1 = f32[6,64,128]{2,0,1:T(8,128)S(1)} async-done(((f32[6,64,128]{2,0,1:T(8,128)}), f32[6,64,128]{2,0,1:T(8,128)S(1)}, u32[]{:S(2)}, u32[]{:S(2)}) %all-to-all-start.1) | async-done | bytes 196640 | tf_op jit(solution)/shard_map/all_to_all | solution.py:96
  77.2 2.6 copy.197
  79.8 51.8 %scatter_fusion.1 = f32[6,4096]{0,1:T(8,128)S(1)} fusion(f32[6,4096]{0,1:T(8,128)S(1)} %scatter_custom_fusion, s32[8192]{0:T(1024)S(1)} %bitcast.43, f32[8192,6]{1,0:T(8,128)} %copy.197), kind=kCustom, calls=%fused_computation.9 | custom fusion | flops 49152 | bytes 622592 | tf_op jit(solution)/shard_map/scatter-add | solution.py:131
  132.3 1.1 broadcast_in_dim.66
  133.3 4.9 all-to-all-start.2
  138.2 16.0 %all-to-all-done.2 = f32[8,6,4096]{2,1,0:T(8,128)S(1)} async-done(((f32[8,6,4096]{2,1,0:T(8,128)}), f32[8,6,4096]{2,1,0:T(8,128)S(1)}, u32[]{:S(2)}, u32[]{:S(2)}) %all-to-all-start.2) | async-done | bytes 786464 | tf_op jit(solution)/shard_map/all_to_all | solution.py:18
  154.3 0.6 copy.200
  154.9 27.7 %gather_fusion.1 = f32[8192,6]{1,0:T(8,128)} fusion(f32[6,4096]{0,1:T(8,128)S(1)} %copy.200, s32[8192]{0:T(1024)S(1)} %broadcast_clamp_fusion), kind=kCustom, calls=%fused_computation.1 | custom fusion | bytes 425984 | tf_op jit(solution)/shard_map/gather | solution.py:142
  182.6 3.5 copy.203
  186.1 4.8 all-to-all-start.3
  191.0 7.3 %gather_fusion = f32[3584,6]{1,0:T(8,128)} fusion(f32[6,4096]{0,1:T(8,128)S(1)} %copy.200, s32[4096]{0:T(1024)S(1)} %pad_clamp_fusion), kind=kCustom, calls=%fused_computation | custom fusion | bytes 186368 | tf_op jit(solution)/shard_map/gather | solution.py:141
  198.3 2.0 copy.201
  200.4 4.7 all-to-all-done.3
  206.5 0.7 multiply_reduce_fusion.12
  207.2 9.5 %all-reduce.5 = (f32[]{:T(128)}, f32[]{:T(128)}) all-reduce(f32[]{:T(128)} %get-tuple-element.40, f32[]{:T(128)} %get-tuple-element.38), channel_id=1, replica_groups=mesh['contact_0'=4,'contact_1'=2,'body'=8,'group'=8] {'contact_0'}, use_global_device_ids=true, to_apply=%region_1.0 | all-reduce | flops 2 | bytes 16 | tf_op jit(solution)/shard_map/psum | solution.py:30
  216.7 3.1 all-reduce.7
  219.8 15.4 %all-reduce.3 = (f32[]{:T(128)}, f32[]{:T(128)}) all-reduce(f32[]{:T(128)} %get-tuple-element.26, f32[]{:T(128)} %get-tuple-element.27), channel_id=1, replica_groups=mesh['contact_0'=4,'contact_1'=2,'body'=8,'group'=8] {'body'}, use_global_device_ids=true, to_apply=%region_3.0 | all-reduce | flops 2 | bytes 16 | tf_op jit(solution)/shard_map/psum | solution.py:30
  235.2 15.9 %all-reduce.1 = (f32[]{:T(128)}, f32[]{:T(128)}) all-reduce(f32[]{:T(128)} %get-tuple-element.18, f32[]{:T(128)} %get-tuple-element.19), channel_id=1, replica_groups=mesh['contact_0'=4,'contact_1'=2,'body'=8,'group'=8] {'group'}, use_global_device_ids=true, to_apply=%region_4.0 | all-reduce | flops 2 | bytes 16 | tf_op jit(solution)/shard_map/psum | solution.py:30
  252.7 0.7 multiply_reduce_fusion.11
  253.7 2.5 scatter_fusion.2
  256.4 0.8 copy.210
  257.2 8.2 %all-to-all-start.4 = ((f32[6,64,128]{2,0,1:T(8,128)}), f32[6,64,128]{2,0,1:T(8,128)S(1)}, u32[]{:S(2)}, u32[]{:S(2)}) async-start(f32[6,64,128]{2,0,1:T(8,128)} %copy.210), calls=%async_computation.4 | async-start | bytes 524288 | tf_op jit(solution)/shard_map/all_to_all | solution.py:96
  265.4 1.8 copy.207
  267.2 20.5 %scatter_custom_fusion.4 = f32[6,4096]{0,1:T(8,128)S(1)} fusion(s32[3584]{0:T(1024)S(1)} %compare_select_fusion.1, f32[3584,6]{1,0:T(8,128)} %copy.207, f32[]{:T(128)} %constant.10.clone.1), kind=kCustom, calls=%fused_computation.18 | custom fusion | flops 21504 | bytes 98816 | tf_op jit(solution)/shard_map/scatter-add | solution.py:126
  287.7 2.6 copy.211
  290.3 51.8 %scatter_fusion.3 = f32[6,4096]{0,1:T(8,128)S(1)} fusion(f32[6,4096]{0,1:T(8,128)S(1)} %scatter_custom_fusion.4, s32[8192]{0:T(1024)S(1)} %bitcast.45, f32[8192,6]{1,0:T(8,128)} %copy.211), kind=kCustom, calls=%fused_computation.12 | custom fusion | flops 49152 | bytes 622592 | tf_op jit(solution)/shard_map/scatter-add | solution.py:131
  342.8 18.8 %all_to_all.45 = f32[8,6,4096]{2,1,0:T(8,128)S(1)} all-to-all(f32[8,6,4096]{2,1,0:T(8,128)S(1)} %broadcast_in_dim.122), channel_id=1, replica_groups=mesh['contact_0'=4,'contact_1'=2,'body'=8,'group'=8] {'contact_0','conta..., dimensions={0} | all-to-all | bytes 1572864 | tf_op jit(solution)/shard_map/all_to_all | solution.py:18
  361.7 0.6 copy.214
  362.3 27.7 %gather_fusion.4 = f32[8192,6]{1,0:T(8,128)} fusion(f32[6,4096]{0,1:T(8,128)S(1)} %copy.214, s32[8192]{0:T(1024)S(1)} %broadcast_clamp_fusion), kind=kCustom, calls=%fused_computation.4 | custom fusion | bytes 425984 | tf_op jit(solution)/shard_map/gather | solution.py:142
  390.0 3.5 copy.217
  393.5 12.5 %all-to-all-start.6 = ((f32[6,64,128]{2,0,1:T(8,128)}), f32[6,64,128]{2,0,1:T(8,128)S(1)}, u32[]{:S(2)}, u32[]{:S(2)}) async-start(f32[6,64,128]{2,0,1:T(8,128)} %copy.217), calls=%async_computation.6 | async-start | bytes 524288 | tf_op jit(solution)/shard_map/all_to_all | solution.py:96
  406.0 7.3 %gather_fusion.3 = f32[3584,6]{1,0:T(8,128)} fusion(f32[6,4096]{0,1:T(8,128)S(1)} %copy.214, s32[4096]{0:T(1024)S(1)} %pad_clamp_fusion), kind=kCustom, calls=%fused_computation.3 | custom fusion | bytes 186368 | tf_op jit(solution)/shard_map/gather | solution.py:141
  413.4 2.0 copy.215
  415.5 4.4 all-to-all-done.6
  421.3 0.6 multiply_reduce_fusion.10
  421.9 9.5 %all-reduce.4 = (f32[]{:T(128)}, f32[]{:T(128)}) all-reduce(f32[]{:T(128)} %get-tuple-element.33, f32[]{:T(128)} %get-tuple-element.31), channel_id=1, replica_groups=mesh['contact_0'=4,'contact_1'=2,'body'=8,'group'=8] {'contact_0'}, use_global_device_ids=true, to_apply=%region_21.22 | all-reduce | flops 2 | bytes 16 | tf_op jit(solution)/shard_map/psum | solution.py:30
  431.4 3.1 all-reduce.6
  434.5 15.4 %all-reduce.2 = (f32[]{:T(128)}, f32[]{:T(128)}) all-reduce(f32[]{:T(128)} %get-tuple-element.24, f32[]{:T(128)} %get-tuple-element.25), channel_id=1, replica_groups=mesh['contact_0'=4,'contact_1'=2,'body'=8,'group'=8] {'body'}, use_global_device_ids=true, to_apply=%region_23.24 | all-reduce | flops 2 | bytes 16 | tf_op jit(solution)/shard_map/psum | solution.py:30
  449.9 15.9 %all-reduce = (f32[]{:T(128)}, f32[]{:T(128)}) all-reduce(f32[]{:T(128)} %get-tuple-element.16, f32[]{:T(128)} %get-tuple-element.17), channel_id=1, replica_groups=mesh['contact_0'=4,'contact_1'=2,'body'=8,'group'=8] {'group'}, use_global_device_ids=true, to_apply=%region_24.25 | all-reduce | flops 2 | bytes 16 | tf_op jit(solution)/shard_map/psum | solution.py:30
  467.8 2.5 scatter_fusion.4
  470.5 0.8 copy.224
  471.3 8.2 %all-to-all-start.7 = ((f32[6,64,128]{2,0,1:T(8,128)}), f32[6,64,128]{2,0,1:T(8,128)S(1)}, u32[]{:S(2)}, u32[]{:S(2)}) async-start(f32[6,64,128]{2,0,1:T(8,128)} %copy.224), calls=%async_computation.7 | async-start | bytes 524288 | tf_op jit(solution)/shard_map/all_to_all | solution.py:96
  479.5 1.8 copy.221
  481.3 20.5 %scatter_custom_fusion.7 = f32[6,4096]{0,1:T(8,128)S(1)} fusion(s32[3584]{0:T(1024)S(1)} %compare_select_fusion.1, f32[3584,6]{1,0:T(8,128)} %copy.221, f32[]{:T(128)} %constant.10.clone.1), kind=kCustom, calls=%fused_computation.16 | custom fusion | flops 21504 | bytes 98816 | tf_op jit(solution)/shard_map/scatter-add | solution.py:126
  501.8 2.6 copy.225
  504.4 51.8 %scatter_fusion.5 = f32[6,4096]{0,1:T(8,128)S(1)} fusion(f32[6,4096]{0,1:T(8,128)S(1)} %scatter_custom_fusion.7, s32[8192]{0:T(1024)S(1)} %bitcast.46, f32[8192,6]{1,0:T(8,128)} %copy.225), kind=kCustom, calls=%fused_computation.15 | custom fusion | flops 49152 | bytes 622592 | tf_op jit(solution)/shard_map/scatter-add | solution.py:131
  556.2 0.6 copy.226
  556.9 18.7 %all_to_all.46 = f32[8,6,4096]{2,1,0:T(8,128)S(1)} all-to-all(f32[8,6,4096]{2,1,0:T(8,128)S(1)} %broadcast_in_dim.126), channel_id=1, replica_groups=mesh['contact_0'=4,'contact_1'=2,'body'=8,'group'=8] {'contact_0','conta..., dimensions={0} | all-to-all | bytes 1572864 | tf_op jit(solution)/shard_map/all_to_all | solution.py:18
  575.7 0.7 multiply_add_fusion
  (76 shorter events, 6.3 us)
Async XLA Ops:
  4.4 46.3 %all-to-all-start = ((s32[1,64,128]{2,0,1:T(1,128)}), s32[1,64,128]{2,0,1:T(1,128)S(1)}, u32[]{:S(2)}, u32[]{:S(2)}) async-start(s32[1,64,128]{2,0,1:T(1,128)} %bitcast.4), calls=%async_computation | async-start | bytes 65536 | tf_op jit(solution)/shard_map/all_to_all | solution.py:118
  50.7 26.5 %all-to-all-start.1 = ((f32[6,64,128]{2,0,1:T(8,128)}), f32[6,64,128]{2,0,1:T(8,128)S(1)}, u32[]{:S(2)}, u32[]{:S(2)}) async-start(f32[6,64,128]{2,0,1:T(8,128)} %copy.196), calls=%async_computation.1 | async-start | bytes 524288 | tf_op jit(solution)/shard_map/all_to_all | solution.py:96
  132.3 22.0 %copy-start = (f32[6,4096]{1,0:T(8,128)S(1)}, f32[6,4096]{1,0:T(8,128)}, u32[]{:S(2)}) copy-start(f32[6,4096]{1,0:T(8,128)} %param.22) | copy-start | bytes 294916
  133.3 20.8 %all-to-all-start.2 = ((f32[8,6,4096]{2,1,0:T(8,128)}), f32[8,6,4096]{2,1,0:T(8,128)S(1)}, u32[]{:S(2)}, u32[]{:S(2)}) async-start(f32[8,6,4096]{2,1,0:T(8,128)} %broadcast_in_dim.66), calls=%async_computation.2 | async-start | bytes 2097152 | tf_op jit(solution)/shard_map/all_to_all | solution.py:18
  186.1 18.9 %all-to-all-start.3 = ((f32[6,64,128]{2,0,1:T(8,128)}), f32[6,64,128]{2,0,1:T(8,128)S(1)}, u32[]{:S(2)}, u32[]{:S(2)}) async-start(f32[6,64,128]{2,0,1:T(8,128)} %copy.203), calls=%async_computation.3 | async-start | bytes 524288 | tf_op jit(solution)/shard_map/all_to_all | solution.py:96
  200.4 6.1 %copy-start.1 = (f32[3,3584]{1,0:T(4,128)S(1)}, f32[3,3584]{1,0:T(4,128)}, u32[]{:S(2)}) copy-start(f32[3,3584]{1,0:T(4,128)} %param.14) | copy-start | bytes 129028
  200.4 6.1 %copy-start.2 = (f32[3,3584]{1,0:T(4,128)S(1)}, f32[3,3584]{1,0:T(4,128)}, u32[]{:S(2)}) copy-start(f32[3,3584]{1,0:T(4,128)} %param.15) | copy-start | bytes 129028
  200.4 6.2 %copy-start.3 = (f32[3,3584]{1,0:T(4,128)S(1)}, f32[3,3584]{1,0:T(4,128)}, u32[]{:S(2)}) copy-start(f32[3,3584]{1,0:T(4,128)} %param.16) | copy-start | bytes 129028
  205.1 47.5 %copy-start.5 = (f32[3584]{0:T(1024)S(1)}, f32[3584]{0:T(1024)}, u32[]{:S(2)}) copy-start(f32[3584]{0:T(1024)} %param.17) | copy-start | bytes 43012
  205.1 47.5 %copy-start.7 = (s32[3584]{0:T(1024)S(1)}, s32[3584]{0:T(1024)}, u32[]{:S(2)}) copy-start(s32[3584]{0:T(1024)} %param.18) | copy-start | bytes 43012
  257.2 30.5 %all-to-all-start.4 = ((f32[6,64,128]{2,0,1:T(8,128)}), f32[6,64,128]{2,0,1:T(8,128)S(1)}, u32[]{:S(2)}, u32[]{:S(2)}) async-start(f32[6,64,128]{2,0,1:T(8,128)} %copy.210), calls=%async_computation.4 | async-start | bytes 524288 | tf_op jit(solution)/shard_map/all_to_all | solution.py:96
  393.5 26.5 %all-to-all-start.6 = ((f32[6,64,128]{2,0,1:T(8,128)}), f32[6,64,128]{2,0,1:T(8,128)S(1)}, u32[]{:S(2)}, u32[]{:S(2)}) async-start(f32[6,64,128]{2,0,1:T(8,128)} %copy.217), calls=%async_computation.6 | async-start | bytes 524288 | tf_op jit(solution)/shard_map/all_to_all | solution.py:96
  467.5 3.0 copy-start.4
  471.3 30.5 %all-to-all-start.7 = ((f32[6,64,128]{2,0,1:T(8,128)}), f32[6,64,128]{2,0,1:T(8,128)S(1)}, u32[]{:S(2)}, u32[]{:S(2)}) async-start(f32[6,64,128]{2,0,1:T(8,128)} %copy.224), calls=%async_computation.7 | async-start | bytes 524288 | tf_op jit(solution)/shard_map/all_to_all | solution.py:96
  556.8 18.9 %copy-start.6 = (f32[6,4096]{1,0:T(8,128)S(1)}, f32[6,4096]{1,0:T(8,128)}, u32[]{:S(2)}) copy-start(f32[6,4096]{1,0:T(8,128)} %param.23) | copy-start | bytes 294916
where the time goes:
time: 578 us; the launch traced here: 576 us
  other arithmetic  224 us (39%)
  blocking collectives  125 us (22%)
  local copies, waits for them, and re-layouts  116 us (20%)
  starting transfers between devices  67.9 us (12%)
  waiting for transfers between devices  38.8 us (7%)
    scatter-add x3, other arithmetic, body_impulse(): summed = summed.at[:, far_index].add(far_terms)  155 us
    psum x8, blocking collectives, by_axis(): array = lax.psum(array, axis)  87.7 us
    scatter-add x3, other arithmetic, body_impulse(): summed = jnp.zeros((6, bodies), jnp.float32).at[:, body_index_a].add(impu...  61.4 us
    gather x2, local copies, waits for them, and re-layouts, on_device(): returned = trade(velocities[:, far_index].reshape(6, shards, -1))  55.4 us
    all_to_all x5, starting transfers between devices, trade(): lax.all_to_all(buffer, ('body', 'group'), split_axis=1, concat_axis=1, ti...  46.4 us
    all_to_all x2, blocking collectives, copy_for_each(): lax.all_to_all(jnp.broadcast_to(array[None], (length, *array.shape)), axi...  37.5 us
    all_to_all x5, waiting for transfers between devices, trade(): lax.all_to_all(buffer, ('body', 'group'), split_axis=1, concat_axis=1, ti...  22.8 us
    gather x4, local copies, waits for them, and re-layouts, on_device(): near_part = velocity_terms(jacobian_a, velocities[:, body_index_a])  18.8 us
  transfers between devices with their start and end apart: 7, of which 4 were waited for; matrix products, arithmetic and copies ran while one was open for 16% of the time, Pallas kernels for 0%

commit v1 on v0

--- a/solution.py
+++ b/solution.py
@@ -11,6 +11,12 @@
 CONTACT_BODY_GROUP = ("contact_0", "contact_1", "body", "group")
 EPS = 1e-06
 SMOOTH = 0.1
+
+
+def add_all(shard, axis):
+    terms = lax.all_gather(shard, axis, axis=0, tiled=False)
+    total = terms.sum(axis=0)
+    return total
 
 
 def copy_for_each(array, axis):
@@ -27,7 +33,7 @@
 
 def by_axis(array, axes):
     for axis in axes:
-        array = lax.psum(array, axis)
+        array = add_all(array, axis)
     return array
 
 

time: 578 us -> 609 us (1.054)
  local copies, waits for them, and re-layouts: 116 us -> 144 us
  other arithmetic: 224 us -> 234 us
    psum x8 -> x0, blocking collectives: 87.7 us -> none  [by_axis(): array = lax.psum(array, axis)]
    unnamed x0 -> x8, blocking collectives: none -> 82.6 us
    unnamed x16 -> x52, local copies, waits for them, and re-layouts: 0.04 us -> 27.6 us
    reduce_sum x0 -> x16, other arithmetic: none -> 9.87 us  [add_all(): total = terms.sum(axis=0)]
where the time goes in v1:
time: 609 us; the launch traced here: 608 us
  other arithmetic  234 us (38%)
  local copies, waits for them, and re-layouts  144 us (24%)
  blocking collectives  120 us (20%)
  starting transfers between devices  69.6 us (11%)
  waiting for transfers between devices  36.2 us (6%)
    scatter-add x3, other arithmetic, body_impulse(): summed = summed.at[:, far_index].add(far_terms)  155 us
    unnamed x8, blocking collectives  82.6 us
    scatter-add x3, other arithmetic, body_impulse(): summed = jnp.zeros((6, bodies), jnp.float32).at[:, body_index_a].add(impu...  61.4 us
    gather x2, local copies, waits for them, and re-layouts, on_device(): returned = trade(velocities[:, far_index].reshape(6, shards, -1))  55.4 us
    all_to_all x5, starting transfers between devices, trade(): lax.all_to_all(buffer, ('body', 'group'), split_axis=1, concat_axis=1, ti...  48.1 us
    all_to_all x2, blocking collectives, copy_for_each(): lax.all_to_all(jnp.broadcast_to(array[None], (length, *array.shape)), axi...  37.5 us
    unnamed x52, local copies, waits for them, and re-layouts  27.6 us
    all_to_all x5, waiting for transfers between devices, trade(): lax.all_to_all(buffer, ('body', 'group'), split_axis=1, concat_axis=1, ti...  20.2 us
  transfers between devices with their start and end apart: 7, of which 4 were waited for; matrix products, arithmetic and copies ran while one was open for 16% of the time, Pallas kernels for 0%

profile of v1, /device:TPU:8, one launch (start us, length us, event | category | flops | bytes accessed | tf_op | source)
XLA Modules:
  0.0 607.9 jit_solution(851980700607022573)
XLA Ops:
  4.4 16.6 %all-to-all-start = ((s32[1,64,128]{2,0,1:T(1,128)}), s32[1,64,128]{2,0,1:T(1,128)S(1)}, u32[]{:S(2)}, u32[]{:S(2)}) async-start(s32[1,64,128]{2,0,1:T(1,128)} %bitcast.12), calls=%async_computation | async-start | bytes 65536 | tf_op jit(solution)/shard_map/all_to_all | solution.py:124
  24.9 2.5 scatter_fusion
  28.4 1.8 copy.192
  30.2 20.5 %scatter_custom_fusion = f32[6,4096]{0,1:T(8,128)S(1)} fusion(s32[3584]{0:T(1024)S(1)} %compare_select_fusion.1, f32[3584,6]{1,0:T(8,128)} %copy.192, f32[]{:T(128)} %constant.10.clone.1), kind=kCustom, calls=%fused_computation.20 | custom fusion | flops 21504 | bytes 98816 | tf_op jit(solution)/shard_map/scatter-add | solution.py:132
  50.7 12.7 %all-to-all-start.1 = ((f32[6,64,128]{2,0,1:T(8,128)}), f32[6,64,128]{2,0,1:T(8,128)S(1)}, u32[]{:S(2)}, u32[]{:S(2)}) async-start(f32[6,64,128]{2,0,1:T(8,128)} %copy.196), calls=%async_computation.1 | async-start | bytes 524288 | tf_op jit(solution)/shard_map/all_to_all | solution.py:102
  63.5 13.7 %all-to-all-done.1 = f32[6,64,128]{2,0,1:T(8,128)S(1)} async-done(((f32[6,64,128]{2,0,1:T(8,128)}), f32[6,64,128]{2,0,1:T(8,128)S(1)}, u32[]{:S(2)}, u32[]{:S(2)}) %all-to-all-start.1) | async-done | bytes 196640 | tf_op jit(solution)/shard_map/all_to_all | solution.py:102
  77.2 2.6 copy.197
  79.8 51.8 %scatter_fusion.1 = f32[6,4096]{0,1:T(8,128)S(1)} fusion(f32[6,4096]{0,1:T(8,128)S(1)} %scatter_custom_fusion, s32[8192]{0:T(1024)S(1)} %bitcast.63, f32[8192,6]{1,0:T(8,128)} %copy.197), kind=kCustom, calls=%fused_computation.9 | custom fusion | flops 49152 | bytes 622592 | tf_op jit(solution)/shard_map/scatter-add | solution.py:137
  133.3 4.9 all-to-all-start.2
  138.2 16.0 %all-to-all-done.2 = f32[8,6,4096]{2,1,0:T(8,128)S(1)} async-done(((f32[8,6,4096]{2,1,0:T(8,128)}), f32[8,6,4096]{2,1,0:T(8,128)S(1)}, u32[]{:S(2)}, u32[]{:S(2)}) %all-to-all-start.2) | async-done | bytes 786464 | tf_op jit(solution)/shard_map/all_to_all | solution.py:24
  154.9 27.7 %gather_fusion.1 = f32[8192,6]{1,0:T(8,128)} fusion(f32[6,4096]{0,1:T(8,128)S(1)} %copy.200, s32[8192]{0:T(1024)S(1)} %broadcast_clamp_fusion), kind=kCustom, calls=%fused_computation.1 | custom fusion | bytes 425984 | tf_op jit(solution)/shard_map/gather | solution.py:148
  182.6 3.5 copy.203
  186.1 4.8 all-to-all-start.3
  190.9 1.3 dynamic-slice
  192.2 7.3 %gather_fusion = f32[3584,6]{1,0:T(8,128)} fusion(f32[6,4096]{0,1:T(8,128)S(1)} %copy.200, s32[4096]{0:T(1024)S(1)} %pad_clamp_fusion), kind=kCustom, calls=%fused_computation | custom fusion | bytes 186368 | tf_op jit(solution)/shard_map/gather | solution.py:147
  199.6 2.0 copy.201
  201.6 3.4 all-to-all-done.3
  207.2 1.3 dynamic-update-slice
  208.5 1.3 dynamic-update-slice.4
  209.8 1.3 dynamic-slice.1
  211.1 8.9 %all-reduce.21 = (f32[4]{0:T(128)S(1)}, f32[4]{0:T(128)S(1)}) all-reduce(f32[4]{0:T(128)S(1)} %dynamic-update-slice, f32[4]{0:T(128)S(1)} %dynamic-update-slice.4), channel_id=1, replica_groups=mesh['contact_0'=4,'contact_1'=2,'body'=8,'group'=8] {'contact_0'}, use_global_device_ids=true, to_apply=%add | all-reduce | flops 8 | bytes 64
  221.3 1.4 dynamic-update-slice.5
  222.7 1.4 dynamic-update-slice.1
  224.1 1.3 dynamic-slice.2
  225.5 2.4 all-reduce.23
  229.2 1.5 dynamic-update-slice.6
  230.7 1.4 dynamic-update-slice.2
  232.1 1.3 dynamic-slice.3
  233.4 14.8 %all-reduce.19 = (f32[8]{0:T(128)S(1)}, f32[8]{0:T(128)S(1)}) all-reduce(f32[8]{0:T(128)S(1)} %dynamic-update-slice.2, f32[8]{0:T(128)S(1)} %dynamic-update-slice.6), channel_id=1, replica_groups=mesh['contact_0'=4,'contact_1'=2,'body'=8,'group'=8] {'body'}, use_global_device_ids=true, to_apply=%add.2 | all-reduce | flops 16 | bytes 128
  249.5 1.4 dynamic-update-slice.7
  250.9 1.4 dynamic-update-slice.3
  252.3 15.3 %all-reduce.17 = (f32[8]{0:T(128)S(1)}, f32[8]{0:T(128)S(1)}) all-reduce(f32[8]{0:T(128)S(1)} %dynamic-update-slice.3, f32[8]{0:T(128)S(1)} %dynamic-update-slice.7), channel_id=1, replica_groups=mesh['contact_0'=4,'contact_1'=2,'body'=8,'group'=8] {'group'}, use_global_device_ids=true, to_apply=%add.3 | all-reduce | flops 16 | bytes 128
  271.3 2.5 scatter_fusion.2
  274.9 8.8 %all-to-all-start.4 = ((f32[6,64,128]{2,0,1:T(8,128)}), f32[6,64,128]{2,0,1:T(8,128)S(1)}, u32[]{:S(2)}, u32[]{:S(2)}) async-start(f32[6,64,128]{2,0,1:T(8,128)} %copy.210), calls=%async_computation.4 | async-start | bytes 524288 | tf_op jit(solution)/shard_map/all_to_all | solution.py:102
  283.6 1.8 copy.207
  285.5 20.5 %scatter_custom_fusion.4 = f32[6,4096]{0,1:T(8,128)S(1)} fusion(s32[3584]{0:T(1024)S(1)} %compare_select_fusion.1, f32[3584,6]{1,0:T(8,128)} %copy.207, f32[]{:T(128)} %constant.10.clone.1), kind=kCustom, calls=%fused_computation.18 | custom fusion | flops 21504 | bytes 98816 | tf_op jit(solution)/shard_map/scatter-add | solution.py:132
  305.9 2.6 copy.211
  308.6 51.8 %scatter_fusion.3 = f32[6,4096]{0,1:T(8,128)S(1)} fusion(f32[6,4096]{0,1:T(8,128)S(1)} %scatter_custom_fusion.4, s32[8192]{0:T(1024)S(1)} %bitcast.65, f32[8192,6]{1,0:T(8,128)} %copy.211), kind=kCustom, calls=%fused_computation.12 | custom fusion | flops 49152 | bytes 622592 | tf_op jit(solution)/shard_map/scatter-add | solution.py:137
  361.1 18.8 %all_to_all.45 = f32[8,6,4096]{2,1,0:T(8,128)S(1)} all-to-all(f32[8,6,4096]{2,1,0:T(8,128)S(1)} %broadcast_in_dim.122), channel_id=1, replica_groups=mesh['contact_0'=4,'contact_1'=2,'body'=8,'group'=8] {'contact_0','conta..., dimensions={0} | all-to-all | bytes 1572864 | tf_op jit(solution)/shard_map/all_to_all | solution.py:24
  380.6 27.7 %gather_fusion.4 = f32[8192,6]{1,0:T(8,128)} fusion(f32[6,4096]{0,1:T(8,128)S(1)} %copy.214, s32[8192]{0:T(1024)S(1)} %broadcast_clamp_fusion), kind=kCustom, calls=%fused_computation.4 | custom fusion | bytes 425984 | tf_op jit(solution)/shard_map/gather | solution.py:148
  408.3 3.5 copy.217
  411.8 12.7 %all-to-all-start.6 = ((f32[6,64,128]{2,0,1:T(8,128)}), f32[6,64,128]{2,0,1:T(8,128)S(1)}, u32[]{:S(2)}, u32[]{:S(2)}) async-start(f32[6,64,128]{2,0,1:T(8,128)} %copy.217), calls=%async_computation.6 | async-start | bytes 524288 | tf_op jit(solution)/shard_map/all_to_all | solution.py:102
  424.5 1.3 dynamic-update-slice.8
  425.8 7.3 %gather_fusion.3 = f32[3584,6]{1,0:T(8,128)} fusion(f32[6,4096]{0,1:T(8,128)S(1)} %copy.214, s32[4096]{0:T(1024)S(1)} %pad_clamp_fusion), kind=kCustom, calls=%fused_computation.3 | custom fusion | bytes 186368 | tf_op jit(solution)/shard_map/gather | solution.py:147
  433.2 2.0 copy.215
  435.4 3.1 all-to-all-done.6
  440.4 1.3 dynamic-update-slice.12
  441.8 8.9 %all-reduce.20 = (f32[4]{0:T(128)S(1)}, f32[4]{0:T(128)S(1)}) all-reduce(f32[4]{0:T(128)S(1)} %dynamic-update-slice.8, f32[4]{0:T(128)S(1)} %dynamic-update-slice.12), channel_id=1, replica_groups=mesh['contact_0'=4,'contact_1'=2,'body'=8,'group'=8] {'contact_0'}, use_global_device_ids=true, to_apply=%add.8 | all-reduce | flops 8 | bytes 64
  451.2 1.4 dynamic-update-slice.13
  453.2 1.4 dynamic-update-slice.9
  454.6 2.4 all-reduce.22
  457.7 1.4 dynamic-update-slice.14
  459.7 1.4 dynamic-update-slice.10
  461.2 14.8 %all-reduce.18 = (f32[8]{0:T(128)S(1)}, f32[8]{0:T(128)S(1)}) all-reduce(f32[8]{0:T(128)S(1)} %dynamic-update-slice.10, f32[8]{0:T(128)S(1)} %dynamic-update-slice.14), channel_id=1, replica_groups=mesh['contact_0'=4,'contact_1'=2,'body'=8,'group'=8] {'body'}, use_global_device_ids=true, to_apply=%add.10 | all-reduce | flops 16 | bytes 128
  476.5 1.4 dynamic-update-slice.15
  478.5 1.4 dynamic-update-slice.11
  479.9 15.2 %all-reduce.16 = (f32[8]{0:T(128)S(1)}, f32[8]{0:T(128)S(1)}) all-reduce(f32[8]{0:T(128)S(1)} %dynamic-update-slice.11, f32[8]{0:T(128)S(1)} %dynamic-update-slice.15), channel_id=1, replica_groups=mesh['contact_0'=4,'contact_1'=2,'body'=8,'group'=8] {'group'}, use_global_device_ids=true, to_apply=%add.11 | all-reduce | flops 16 | bytes 128
  498.3 2.5 scatter_fusion.4
  501.8 9.1 %all-to-all-start.7 = ((f32[6,64,128]{2,0,1:T(8,128)}), f32[6,64,128]{2,0,1:T(8,128)S(1)}, u32[]{:S(2)}, u32[]{:S(2)}) async-start(f32[6,64,128]{2,0,1:T(8,128)} %copy.224), calls=%async_computation.7 | async-start | bytes 524288 | tf_op jit(solution)/shard_map/all_to_all | solution.py:102
  510.9 1.8 copy.221
  512.8 20.5 %scatter_custom_fusion.7 = f32[6,4096]{0,1:T(8,128)S(1)} fusion(s32[3584]{0:T(1024)S(1)} %compare_select_fusion.1, f32[3584,6]{1,0:T(8,128)} %copy.221, f32[]{:T(128)} %constant.10.clone.1), kind=kCustom, calls=%fused_computation.16 | custom fusion | flops 21504 | bytes 98816 | tf_op jit(solution)/shard_map/scatter-add | solution.py:132
  533.2 2.6 copy.225
  535.9 51.8 %scatter_fusion.5 = f32[6,4096]{0,1:T(8,128)S(1)} fusion(f32[6,4096]{0,1:T(8,128)S(1)} %scatter_custom_fusion.7, s32[8192]{0:T(1024)S(1)} %bitcast.66, f32[8192,6]{1,0:T(8,128)} %copy.225), kind=kCustom, calls=%fused_computation.15 | custom fusion | flops 49152 | bytes 622592 | tf_op jit(solution)/shard_map/scatter-add | solution.py:137
  588.4 18.7 %all_to_all.46 = f32[8,6,4096]{2,1,0:T(8,128)S(1)} all-to-all(f32[8,6,4096]{2,1,0:T(8,128)S(1)} %broadcast_in_dim.126), channel_id=1, replica_groups=mesh['contact_0'=4,'contact_1'=2,'body'=8,'group'=8] {'contact_0','conta..., dimensions={0} | all-to-all | bytes 1572864 | tf_op jit(solution)/shard_map/all_to_all | solution.py:24
  (128 shorter events, 31.8 us)
Async XLA Ops:
  4.4 46.3 %all-to-all-start = ((s32[1,64,128]{2,0,1:T(1,128)}), s32[1,64,128]{2,0,1:T(1,128)S(1)}, u32[]{:S(2)}, u32[]{:S(2)}) async-start(s32[1,64,128]{2,0,1:T(1,128)} %bitcast.12), calls=%async_computation | async-start | bytes 65536 | tf_op jit(solution)/shard_map/all_to_all | solution.py:124
  50.7 26.5 %all-to-all-start.1 = ((f32[6,64,128]{2,0,1:T(8,128)}), f32[6,64,128]{2,0,1:T(8,128)S(1)}, u32[]{:S(2)}, u32[]{:S(2)}) async-start(f32[6,64,128]{2,0,1:T(8,128)} %copy.196), calls=%async_computation.1 | async-start | bytes 524288 | tf_op jit(solution)/shard_map/all_to_all | solution.py:102
  132.3 22.0 %copy-start = (f32[6,4096]{1,0:T(8,128)S(1)}, f32[6,4096]{1,0:T(8,128)}, u32[]{:S(2)}) copy-start(f32[6,4096]{1,0:T(8,128)} %param.22) | copy-start | bytes 294916
  133.3 20.8 %all-to-all-start.2 = ((f32[8,6,4096]{2,1,0:T(8,128)}), f32[8,6,4096]{2,1,0:T(8,128)S(1)}, u32[]{:S(2)}, u32[]{:S(2)}) async-start(f32[8,6,4096]{2,1,0:T(8,128)} %broadcast_in_dim.66), calls=%async_computation.2 | async-start | bytes 2097152 | tf_op jit(solution)/shard_map/all_to_all | solution.py:24
  186.1 18.9 %all-to-all-start.3 = ((f32[6,64,128]{2,0,1:T(8,128)}), f32[6,64,128]{2,0,1:T(8,128)S(1)}, u32[]{:S(2)}, u32[]{:S(2)}) async-start(f32[6,64,128]{2,0,1:T(8,128)} %copy.203), calls=%async_computation.3 | async-start | bytes 524288 | tf_op jit(solution)/shard_map/all_to_all | solution.py:102
  201.6 4.9 copy-start.1
  201.6 4.9 copy-start.2
  201.6 4.9 copy-start.3
  205.1 65.2 %copy-start.5 = (f32[3584]{0:T(1024)S(1)}, f32[3584]{0:T(1024)}, u32[]{:S(2)}) copy-start(f32[3584]{0:T(1024)} %param.17) | copy-start | bytes 43012
  205.1 65.2 %copy-start.7 = (s32[3584]{0:T(1024)S(1)}, s32[3584]{0:T(1024)}, u32[]{:S(2)}) copy-start(s32[3584]{0:T(1024)} %param.18) | copy-start | bytes 43012
  274.9 31.1 %all-to-all-start.4 = ((f32[6,64,128]{2,0,1:T(8,128)}), f32[6,64,128]{2,0,1:T(8,128)S(1)}, u32[]{:S(2)}, u32[]{:S(2)}) async-start(f32[6,64,128]{2,0,1:T(8,128)} %copy.210), calls=%async_computation.4 | async-start | bytes 524288 | tf_op jit(solution)/shard_map/all_to_all | solution.py:102
  411.8 26.7 %all-to-all-start.6 = ((f32[6,64,128]{2,0,1:T(8,128)}), f32[6,64,128]{2,0,1:T(8,128)S(1)}, u32[]{:S(2)}, u32[]{:S(2)}) async-start(f32[6,64,128]{2,0,1:T(8,128)} %copy.217), calls=%async_computation.6 | async-start | bytes 524288 | tf_op jit(solution)/shard_map/all_to_all | solution.py:102
  498.0 3.0 copy-start.4
  501.8 31.4 %all-to-all-start.7 = ((f32[6,64,128]{2,0,1:T(8,128)}), f32[6,64,128]{2,0,1:T(8,128)S(1)}, u32[]{:S(2)}, u32[]{:S(2)}) async-start(f32[6,64,128]{2,0,1:T(8,128)} %copy.224), calls=%async_computation.7 | async-start | bytes 524288 | tf_op jit(solution)/shard_map/all_to_all | solution.py:102
  588.3 18.9 %copy-start.6 = (f32[6,4096]{1,0:T(8,128)S(1)}, f32[6,4096]{1,0:T(8,128)}, u32[]{:S(2)}) copy-start(f32[6,4096]{1,0:T(8,128)} %param.23) | copy-start | bytes 294916
